TPU v7x, 32 devices: a whole 2x2x4 slice. The times are simulated.
32 devices in a mesh: freq: 8 (over z, x), pol: 2 (over core), beam: 2 (over y).
Axes of the slice: x: 2, y: 2, z: 4, core: 2. Of those that a mesh axis runs over, the one named last changes fastest.
Arguments:
- voltages: bfloat16 [1024, 2, 256, 512], P('freq', 'pol', 'beam'), may hold values from -6 to 6
- beam_weights: bfloat16 [256, 2, 1024, 512], P('freq', None, None, 'beam'), may hold values from -0.125 to 0.125
- delay_shifts: int32 [8, 256], replicated, may hold values from 0 to 255, as said below
Outputs:
- dedispersed: float32 [256, 2, 256, 256], P('freq', 'beam', 'pol')
Inputs may be any that keep to these rules, and one draw needn't show every extreme that they name: delay_shifts[s, d] lies between (d + 1) // 2 and d; only entries with d below 2 ** (s + 1) are read.
All inputs are finite; a program needn't handle non-finite values.
Results may differ from a plain program's by a relative error of at most 0.0006.
Values may be sent and summed in bfloat16 or wider, within the bound.
A program may use at most 256 MiB of HBM per device.

v0:
```python
import math
import jax
import jax.numpy as jnp
from jax import lax
from jax.sharding import PartitionSpec as P

F = 256


def swapped(shard, axis, bit):
    return lax.ppermute(shard, axis, [(i, i ^ 1 << bit) for i in range(lax.axis_size(axis))])


def fourier_table(length):
    index_row = jnp.arange(length, dtype=jnp.int32)
    product = index_row[:, None] * index_row[None, :] % length
    phase_angle = 2.0 * math.pi / length * product.astype(jnp.float32)
    norm_scale = 1.0 / math.sqrt(length)
    cosine = jnp.cos(phase_angle) * norm_scale
    sine_part = jnp.sin(phase_angle) * norm_scale
    real_rows = jnp.concatenate([cosine, sine_part], axis=1)
    imag_rows = jnp.concatenate([-sine_part, cosine], axis=1)
    return jnp.concatenate([real_rows, imag_rows], axis=0).astype(jnp.bfloat16)


def shift_rows(planes, amounts):
    length = planes.shape[-1]
    padded = jnp.concatenate([planes, jnp.zeros_like(planes)], axis=-1)
    return jax.vmap(
        lambda single_plane, amount: lax.dynamic_slice_in_dim(single_plane, amount, length, axis=1)
    )(padded, amounts)


def merge_level(planes, shift_row):
    first_half = planes[0::2]
    second_half = planes[1::2]
    widened = 2 * planes.shape[1]
    first_rep = jnp.repeat(first_half, 2, axis=1)
    second_rep = jnp.repeat(second_half, 2, axis=1)
    amounts = shift_row[:widened]
    shifted = jax.vmap(shift_rows, in_axes=(0, None))(second_rep, amounts)
    return first_rep + shifted


def contract(weights_part, volts_part):
    return jnp.einsum("cab,cas->cbs", weights_part, volts_part, preferred_element_type=jnp.float32)


def beam_power(real_weights, imag_weights, real_volts, imag_volts):
    real_beam = contract(real_weights, real_volts) - contract(imag_weights, imag_volts)
    imag_beam = contract(imag_weights, real_volts) + contract(real_weights, imag_volts)
    return real_beam * real_beam + imag_beam * imag_beam


def per_device(voltages, beam_weights, delay_shifts):
    freq_count = lax.axis_size("freq")
    beam_count = lax.axis_size("beam")
    rows_each = beam_weights.shape[0]
    fourier = fourier_table(F)
    channelized = lax.dot_general(
        fourier, voltages, (((1,), (3,)), ((), ())), preferred_element_type=jnp.float32
    )
    channelized = channelized.astype(jnp.bfloat16).reshape(
        2, F, voltages.shape[0], voltages.shape[2]
    )
    turned = lax.all_to_all(channelized, "freq", split_axis=1, concat_axis=2, tiled=True)
    piece = lax.all_gather(beam_weights, "beam", axis=3, tiled=True)
    powers = beam_power(piece[:, 0], piece[:, 1], turned[0], turned[1])
    grouped = powers.reshape(
        powers.shape[0], beam_count, powers.shape[1] // beam_count, powers.shape[2]
    )
    halved = lax.psum_scatter(
        grouped.astype(jnp.bfloat16), "pol", scatter_dimension=2, tiled=True
    ).astype(jnp.float32)
    regrouped = lax.all_to_all(
        halved.astype(jnp.bfloat16), "beam", split_axis=1, concat_axis=3, tiled=True
    ).astype(halved.dtype)
    summed = regrouped[:, 0]
    planes = summed[:, None]
    local_levels = rows_each.bit_length() - 1
    for level_index in range(local_levels):
        planes = merge_level(planes, delay_shifts[level_index])
    held_rows = planes[0]
    device = lax.axis_index("freq")
    position = jnp.zeros((), jnp.int32)
    half_rows = rows_each // 2
    for section_index in range(freq_count.bit_length() - 1):
        level_now = local_levels + section_index
        high_bit = device // 2**section_index % 2
        lower_side = high_bit == 0
        outgoing = jnp.where(lower_side, held_rows[half_rows:], held_rows[:half_rows])
        received = swapped(outgoing, "freq", section_index)
        first_rows = jnp.where(lower_side, held_rows[:half_rows], received)
        second_rows = jnp.where(lower_side, received, held_rows[half_rows:])
        position = 2 * position + high_bit
        amounts = lax.dynamic_slice_in_dim(delay_shifts[level_now], position * rows_each, rows_each)
        held_rows = jnp.repeat(first_rows, 2, axis=0) + shift_rows(
            jnp.repeat(second_rows, 2, axis=0), amounts
        )
    return (held_rows * (1.0 / (4 * F)))[:, None]


def solution(mesh):
    in_specs = (P("freq", "pol", "beam", None), P("freq", None, None, "beam"), P())
    out_specs = P("freq", "beam", "pol", None)
    return jax.shard_map(
        per_device, mesh=mesh, in_specs=in_specs, out_specs=out_specs, check_vma=False
    )
```

profile of v0, /device:TPU:0, one launch (start us, length us, event | category | flops | bytes accessed | tf_op | source)
XLA Modules:
  0.0 1500.7 jit_solution(10982855420951814088)
XLA Ops:
  6.5 22.9 %copy.25 = bf16[32,2,1024,256]{3,2,0,1:T(8,128)(2,1)} copy(bf16[32,2,1024,256]{3,2,1,0:T(8,128)(2,1)} %param.4) | data formatting | bytes 67108864 | tf_op args[1]
  31.6 24.3 %fusion.6 = bf16[512,128,128]{2,0,1:T(8,128)(2,1)} fusion(bf16[128,1,128,512]{3,2,1,0:T(8,128)(2,1)} %param.3, bf16[256,256]{1,0:T(8,128)(2,1)S(1)} %get-tuple-element.21, bf16[256,256]{1,0:T(8,128)(2,1)S(1)} %get-tuple-element.20, bf16[256,256]{1,0:T(8,128)(2,1)S(1)} %fusion.26), kind=kOutput, calls=%fused_computation.16 | convolution fusion | flops 8600420352 | bytes 33947648 | tf_op jit(solution)/shard_map/dot_general | solution.py:60
  55.9 23.5 %copy.23 = bf16[2,256,128,128]{3,0,2,1:T(2,128)(2,1)S(1)} copy(bf16[2,256,128,128]{3,1,0,2:T(8,128)(2,1)} %bitcast.158) | data formatting | bytes 33554432 | tf_op jit(solution)/shard_map/reshape | solution.py:63
  79.5 370.4 %all_to_all.24 = bf16[2,256,128,128]{3,0,2,1:T(2,128)(2,1)} all-to-all(bf16[2,256,128,128]{3,0,2,1:T(2,128)(2,1)S(1)} %copy.23), channel_id=1, replica_groups=mesh['freq'=8,'pol'=2,'beam'=2] {'freq'}, dimensions={1} | all-to-all | bytes 33554432 | tf_op jit(solution)/shard_map/all_to_all | solution.py:66
  449.9 27.9 %copy.24 = bf16[2,8,32,128,128]{3,1,4,2,0:T(8,128)(2,1)} copy(bf16[2,8,32,128,128]{4,0,3,2,1:T(2,128)(2,1)} %bitcast.152) | data formatting | bytes 33554432 | tf_op jit(solution)/shard_map/all_to_all | solution.py:66
  477.8 11.6 fusion.51
  489.4 13.3 squeeze.10
  502.7 13.3 squeeze.8
  516.0 284.2 %all-gather.2.cloned.1.call-done = bf16[32,2,1024,512]{3,2,0,1:T(8,128)(2,1)} async-done(((bf16[32,2,1024,256]{3,2,0,1:T(8,128)(2,1)}), bf16[32,2,1024,512]{3,2,0,1:T(8,128)(2,1)}) %all-gather.2.cloned.1.call-update) | async-done | bytes 67108880 | tf_op jit(solution)/shard_map/all_gather | solution.py:67
  800.2 19.4 %fusion.1 = f32[32,128,512]{2,1,0:T(8,128)} fusion(bf16[32,1024,128]{1,2,0:T(8,128)(2,1)} %squeeze.8, bf16[32,2,1024,512]{3,2,0,1:T(8,128)(2,1)} %all-gather.2.cloned.1.call-done), kind=kOutput, calls=%fused_computation.11 | convolution fusion | flops 4294967296 | bytes 50331648 | tf_op jit(solution)/shard_map/cab,cas->cbs/dot_general | solution.py:46
  819.6 19.4 %fusion.2 = f32[32,128,512]{2,1,0:T(8,128)} fusion(bf16[32,1024,128]{1,2,0:T(8,128)(2,1)} %squeeze.8, bf16[32,2,1024,512]{3,2,0,1:T(8,128)(2,1)} %all-gather.2.cloned.1.call-done), kind=kOutput, calls=%fused_computation.12 | convolution fusion | flops 4294967296 | bytes 50331648 | tf_op jit(solution)/shard_map/cab,cas->cbs/dot_general | solution.py:46
  839.0 19.4 %fusion = f32[32,128,512]{2,1,0:T(8,128)} fusion(bf16[32,1024,128]{1,2,0:T(8,128)(2,1)} %squeeze.10, bf16[32,2,1024,512]{3,2,0,1:T(8,128)(2,1)} %all-gather.2.cloned.1.call-done), kind=kOutput, calls=%fused_computation.10 | convolution fusion | flops 4294967296 | bytes 50331648 | tf_op jit(solution)/shard_map/cab,cas->cbs/dot_general | solution.py:46
  858.4 25.0 %fusion.9 = bf16[32,512,128]{1,2,0:T(8,128)(2,1)} fusion(f32[32,128,512]{2,1,0:T(8,128)} %fusion.2, f32[32,128,512]{2,1,0:T(8,128)} %fusion, f32[32,128,512]{2,1,0:T(8,128)} %fusion.1, bf16[32,1024,128]{1,2,0:T(8,128)(2,1)} %squeeze.10, bf16[32,2,1024,512]{3,2,0,1:T(8,128)(2,1)} %all-gather.2.cloned.1.call-done), kind=kOutput, calls=%fused_computation.19 | convolution fusion | flops 4307550208 | bytes 71303168 | tf_op jit(solution)/shard_map/cab,cas->cbs/dot_general | solution.py:46
  890.3 14.7 copy.37
  913.5 11.5 reduce-scatter.4.cloned.1.call-done
  936.4 25.4 %all-to-all-done.1 = bf16[32,2,128,128]{2,3,0,1:T(8,128)(2,1)S(1)} async-done(((bf16[32,2,128,128]{2,3,0,1:T(8,128)(2,1)}), bf16[32,2,128,128]{2,3,0,1:T(8,128)(2,1)S(1)}, u32[]{:S(2)}, u32[]{:S(2)}) %all-to-all-start.1) | async-done | bytes 2097184 | tf_op jit(solution)/shard_map/all_to_all | solution.py:75
  980.6 11.5 slice.144
  992.1 10.0 slice.143
  1019.5 21.4 %slice.148 = f32[4,4,128,256]{2,0,3,1:T(4,128)} slice(f32[8,4,128,256]{2,0,3,1:T(8,128)} %bitcast_add_fusion.4), slice={[1:8:2], [0:4:1], [0:128:1], [0:256:1]} | slice | bytes 4194304 | tf_op jit(solution)/shard_map/slice | solution.py:36
  1040.9 19.6 %slice.147 = f32[4,4,128,256]{2,0,3,1:T(4,128)S(1)} slice(f32[8,4,128,256]{2,0,3,1:T(8,128)} %bitcast_add_fusion.4), slice={[0:8:2], [0:4:1], [0:128:1], [0:256:1]} | slice | bytes 4194304 | tf_op jit(solution)/shard_map/slice | solution.py:35
  1068.4 9.0 gather_fusion.2
  1082.5 39.5 %slice.152 = f32[2,8,128,256]{2,0,3,1:T(2,128)} slice(f32[4,8,128,256]{2,0,3,1:T(4,128)} %bitcast_add_fusion.3), slice={[1:4:2], [0:8:1], [0:128:1], [0:256:1]} | slice | bytes 4194304 | tf_op jit(solution)/shard_map/slice | solution.py:36
  1122.0 36.5 %slice.151 = f32[2,8,128,256]{2,0,3,1:T(2,128)S(1)} slice(f32[4,8,128,256]{2,0,3,1:T(4,128)} %bitcast_add_fusion.3), slice={[0:4:2], [0:8:1], [0:128:1], [0:256:1]} | slice | bytes 4194304 | tf_op jit(solution)/shard_map/slice | solution.py:35
  1164.1 9.6 concatenate.69
  1173.8 11.9 gather_fusion.3
  1203.4 10.3 gather_fusion.4
  1223.0 45.4 %collective-permute-done = f32[16,128,256]{1,0,2:T(8,128)} collective-permute-done((f32[16,128,256]{1,0,2:T(8,128)S(1)}, f32[16,128,256]{1,0,2:T(8,128)}, u32[]{:S(2)}, u32[]{:S(2)}) %collective-permute-start) | collective-permute-done | bytes 2097184 | tf_op jit(solution)/shard_map/ppermute | solution.py:11
  1279.9 10.1 gather_fusion.5
  1299.6 44.7 %collective-permute-done.1 = f32[16,128,256]{1,0,2:T(8,128)} collective-permute-done((f32[16,128,256]{1,0,2:T(8,128)S(1)}, f32[16,128,256]{1,0,2:T(8,128)}, u32[]{:S(2)}, u32[]{:S(2)}) %collective-permute-start.1) | collective-permute-done | bytes 2097184 | tf_op jit(solution)/shard_map/ppermute | solution.py:11
  1355.6 10.1 gather_fusion.6
  1373.6 88.9 %collective-permute-done.2 = f32[16,128,256]{1,0,2:T(8,128)S(1)} collective-permute-done((f32[16,128,256]{1,0,2:T(8,128)S(1)}, f32[16,128,256]{1,0,2:T(8,128)S(1)}, u32[]{:S(2)}, u32[]{:S(2)}) %collective-permute-start.2) | collective-permute-done | bytes 2097184 | tf_op jit(solution)/shard_map/ppermute | solution.py:11
  1471.1 10.1 gather_fusion.7
  (81 shorter events, 171.9 us)
Async XLA Ops:
  6.5 793.7 %all-gather.2.cloned.1.call-start = ((), (), s32[]{:S(2)}) async-start(), calls=%async_computation.3 | async-start | bytes 100663296 | tf_op jit(solution)/shard_map/all_gather | solution.py:67
  29.4 895.6 %reduce-scatter.4.cloned.1.call-start = ((), (), s32[]{:S(2)}) async-start(), calls=%async_computation.4 | async-start | bytes 6291456
  912.8 0.7 copy-start.6
  932.5 29.3 %all-to-all-start.1 = ((bf16[32,2,128,128]{2,3,0,1:T(8,128)(2,1)}), bf16[32,2,128,128]{2,3,0,1:T(8,128)(2,1)S(1)}, u32[]{:S(2)}, u32[]{:S(2)}) async-start(bf16[32,2,128,128]{2,3,0,1:T(8,128)(2,1)} %copy.27), calls=%async_computation.1 | async-start | bytes 4194304 | tf_op jit(solution)/shard_map/all_to_all | solution.py:75
  1213.8 4.2 copy-start.5
  1219.0 2.0 copy-start.1
  1221.3 47.2 %collective-permute-start = (f32[16,128,256]{1,0,2:T(8,128)S(1)}, f32[16,128,256]{1,0,2:T(8,128)}, u32[]{:S(2)}, u32[]{:S(2)}) collective-permute-start(f32[16,128,256]{1,0,2:T(8,128)S(1)} %fusion.12), channel_id=1, source_target_pairs={{0,4},{4,0},{8,12},{12,8},{16,20},{20,16},{24,28},{28,24},{1,5},{5... | collective-permute-start | bytes 6291464 | tf_op jit(solution)/shard_map/ppermute | solution.py:11
  1290.0 4.2 copy-start.2
  1295.6 2.0 copy-start
  1297.9 46.3 %collective-permute-start.1 = (f32[16,128,256]{1,0,2:T(8,128)S(1)}, f32[16,128,256]{1,0,2:T(8,128)}, u32[]{:S(2)}, u32[]{:S(2)}) collective-permute-start(f32[16,128,256]{1,0,2:T(8,128)S(1)} %slice_select_fusion.4), channel_id=1, source_target_pairs={{0,8},{4,12},{8,0},{12,4},{16,24},{20,28},{24,16},{28,20},{1,9},{5... | collective-permute-start | bytes 6291464 | tf_op jit(solution)/shard_map/ppermute | solution.py:11
  1365.7 4.2 copy-start.3
  1371.3 91.2 %collective-permute-start.2 = (f32[16,128,256]{1,0,2:T(8,128)S(1)}, f32[16,128,256]{1,0,2:T(8,128)S(1)}, u32[]{:S(2)}, u32[]{:S(2)}) collective-permute-start(f32[16,128,256]{1,0,2:T(8,128)S(1)} %slice_select_fusion.1), channel_id=1, source_target_pairs={{0,16},{4,20},{8,24},{12,28},{16,0},{20,4},{24,8},{28,12},{1,17},{... | collective-permute-start | bytes 6291464 | tf_op jit(solution)/shard_map/ppermute | solution.py:11
  1481.2 4.2 copy-start.4
Sparse Core Ops, SparseCore 0:
  29.5 770.6 all-gather.1
  912.9 12.0 reduce-scatter.3
where the time goes:
time: 1520 us; the launch traced here: 1500 us
  waiting for transfers between devices  500 us (33%)
  local copies, waits for them, and re-layouts  460 us (30%)
  blocking collectives  370 us (24%)
  matrix products  108 us (7%)
  other arithmetic  39.6 us (3%)
    all_to_all x1, blocking collectives, per_device(): lax.all_to_all(channelized, 'freq', split_axis=1, concat_axis=2, tiled=True)  370 us
    all_gather x1, waiting for transfers between devices, per_device(): piece = lax.all_gather(beam_weights, 'beam', axis=3, tiled=True)  284 us
    ppermute x3, waiting for transfers between devices, swapped(): lax.ppermute(shard, axis, [(i, i ^ 1 << bit) for i in range(lax.axis_size...  179 us
    slice x9, local copies, waits for them, and re-layouts, merge_level(): second_half = planes[1::2]  84 us
    dot_general x4, matrix products, contract(): jnp.einsum('cab,cas->cbs', weights_part, volts_part, preferred_element_ty...  83.2 us
    gather x8, local copies, waits for them, and re-layouts, shift_rows(): lax.dynamic_slice_in_dim(single_plane, amount, length, axis=1)  74.2 us
    slice x6, local copies, waits for them, and re-layouts, merge_level(): first_half = planes[0::2]  70.3 us
    unnamed x18, local copies, waits for them, and re-layouts  53.4 us
  transfers between devices with their start and end apart: 6, of which 6 were waited for; matrix products, arithmetic and copies ran while one was open for 8% of the time, Pallas kernels for 0%

commit v1 on v0

--- a/solution.py
+++ b/solution.py
@@ -63,7 +63,15 @@
     channelized = channelized.astype(jnp.bfloat16).reshape(
         2, F, voltages.shape[0], voltages.shape[2]
     )
-    turned = lax.all_to_all(channelized, "freq", split_axis=1, concat_axis=2, tiled=True)
+    ways, here = (lax.axis_size("freq"), lax.axis_index("freq"))
+    width = channelized.shape[1] // ways
+    turned_2 = jnp.roll(channelized, -here * width, axis=1)
+    got = [lax.slice_in_dim(turned_2, 0, width, axis=1)]
+    for far in range(1, ways):
+        sent = lax.slice_in_dim(turned_2, far * width, (far + 1) * width, axis=1)
+        got.append(lax.ppermute(sent, "freq", [(d, (d + far) % ways) for d in range(ways)]))
+    line = jnp.concatenate(got[::-1], axis=2)
+    turned = jnp.roll(line, (here + 1) * got[0].shape[2], axis=2)
     piece = lax.all_gather(beam_weights, "beam", axis=3, tiled=True)
     powers = beam_power(piece[:, 0], piece[:, 1], turned[0], turned[1])
     grouped = powers.reshape(

time: 1520 us -> 1520 us (level)
  blocking collectives: 370 us -> 0 us
  waiting for transfers between devices: 500 us -> 856 us
    all_to_all x1 -> x0, blocking collectives: 370 us -> none  [per_device(): lax.all_to_all(channelized, 'freq', split_axis=1, concat_axis=2, tiled=True)]
    ppermute x0 -> x7, waiting for transfers between devices: none -> 347 us  [per_device(): lax.ppermute(sent, 'freq', [(d, (d + far) % ways) for d in range(ways)])]
    unnamed x18 -> x35, local copies, waits for them, and re-layouts: 53.4 us -> 102 us
    all_to_all x1 -> x0, local copies, waits for them, and re-layouts: 27.9 us -> none  [per_device(): lax.all_to_all(channelized, 'freq', split_axis=1, concat_axis=2, tiled=True)]
    squeeze x2 -> x0, local copies, waits for them, and re-layouts: 26.6 us -> none  [per_device(): powers = beam_power(piece[:, 0], piece[:, 1], turned[0], turned[1])]
  transfers between devices with their start and end apart: 6 -> 13, of which waited for: 6 -> 10; matrix products, arithmetic and copies ran while one was open for 8% -> 8% of each run, Pallas kernels for 0% -> 0%
where the time goes in v1:
time: 1520 us; the launch traced here: 1500 us
  waiting for transfers between devices  856 us (56%)
  local copies, waits for them, and re-layouts  454 us (30%)
  matrix products  107 us (7%)
  other arithmetic  50.4 us (3%)
  starting transfers between devices  19.5 us (1%)
    ppermute x7, waiting for transfers between devices, per_device(): lax.ppermute(sent, 'freq', [(d, (d + far) % ways) for d in range(ways)])  347 us
    all_gather x1, waiting for transfers between devices, per_device(): piece = lax.all_gather(beam_weights, 'beam', axis=3, tiled=True)  293 us
    ppermute x3, waiting for transfers between devices, swapped(): lax.ppermute(shard, axis, [(i, i ^ 1 << bit) for i in range(lax.axis_size...  179 us
    unnamed x35, local copies, waits for them, and re-layouts  102 us
    slice x9, local copies, waits for them, and re-layouts, merge_level(): second_half = planes[1::2]  84.1 us
    dot_general x4, matrix products, contract(): jnp.einsum('cab,cas->cbs', weights_part, volts_part, preferred_element_ty...  82.2 us
    gather x8, local copies, waits for them, and re-layouts, shift_rows(): lax.dynamic_slice_in_dim(single_plane, amount, length, axis=1)  74.2 us
    slice x6, local copies, waits for them, and re-layouts, merge_level(): first_half = planes[0::2]  70.3 us
  transfers between devices with their start and end apart: 13, of which 10 were waited for; matrix products, arithmetic and copies ran while one was open for 8% of the time, Pallas kernels for 0%

profile of v1, /device:TPU:0, one launch (start us, length us, event | category | flops | bytes accessed | tf_op | source)
XLA Modules:
  0.0 1499.7 jit_solution(10004434868820856724)
XLA Ops:
  6.5 22.9 %copy.27 = bf16[32,2,1024,256]{3,2,0,1:T(8,128)(2,1)} copy(bf16[32,2,1024,256]{3,2,1,0:T(8,128)(2,1)} %param.4) | data formatting | bytes 67108864 | tf_op args[1]
  31.6 24.4 %fusion.7 = bf16[512,128,128]{2,0,1:T(8,128)(2,1)} fusion(bf16[128,1,128,512]{3,2,1,0:T(8,128)(2,1)} %param.3, bf16[256,256]{1,0:T(8,128)(2,1)S(1)} %get-tuple-element.30, bf16[256,256]{1,0:T(8,128)(2,1)S(1)} %get-tuple-element.29, bf16[256,256]{1,0:T(8,128)(2,1)S(1)} %fusion.27), kind=kOutput, calls=%fused_computation.19 | convolution fusion | flops 8600420352 | bytes 33947648 | tf_op jit(solution)/shard_map/dot_general | solution.py:60
  56.0 25.4 %copy.25 = bf16[2,256,128,128]{2,3,1,0:T(8,128)(2,1)} copy(bf16[2,256,128,128]{3,1,0,2:T(8,128)(2,1)} %bitcast.152) | data formatting | bytes 33554432 | tf_op jit(solution)/shard_map/reshape | solution.py:63
  81.4 11.0 fusion.4
  111.3 42.6 %collective-permute-done = bf16[2,32,128,128]{2,3,1,0:T(8,128)(2,1)S(1)} collective-permute-done((bf16[2,32,128,128]{2,3,1,0:T(8,128)(2,1)S(1)}, bf16[2,32,128,128]{2,3,1,0:T(8,128)(2,1)S(1)}, u32[]{:S(2)}, u32[]{:S(2)}) %collective-permute-start) | collective-permute-done | bytes 2097184 | tf_op jit(solution)/shard_map/ppermute | solution.py:72
  153.9 44.9 %collective-permute-done.1 = bf16[2,32,128,128]{2,3,1,0:T(8,128)(2,1)} collective-permute-done((bf16[2,32,128,128]{2,3,1,0:T(8,128)(2,1)S(1)}, bf16[2,32,128,128]{2,3,1,0:T(8,128)(2,1)}, u32[]{:S(2)}, u32[]{:S(2)}) %collective-permute-start.1) | collective-permute-done | bytes 2097184 | tf_op jit(solution)/shard_map/ppermute | solution.py:72
  203.7 40.2 %collective-permute-done.2 = bf16[2,32,128,128]{2,3,1,0:T(8,128)(2,1)} collective-permute-done((bf16[2,32,128,128]{2,3,1,0:T(8,128)(2,1)}, bf16[2,32,128,128]{2,3,1,0:T(8,128)(2,1)}, u32[]{:S(2)}, u32[]{:S(2)}) %collective-permute-start.2) | collective-permute-done | bytes 2097184 | tf_op jit(solution)/shard_map/ppermute | solution.py:72
  247.3 219.6 %collective-permute-done.3 = bf16[2,32,128,128]{2,3,1,0:T(8,128)(2,1)} collective-permute-done((bf16[2,32,128,128]{2,3,1,0:T(8,128)(2,1)}, bf16[2,32,128,128]{2,3,1,0:T(8,128)(2,1)}, u32[]{:S(2)}, u32[]{:S(2)}) %collective-permute-start.3) | collective-permute-done | bytes 2097184 | tf_op jit(solution)/shard_map/ppermute | solution.py:72
  507.6 292.6 %all-gather.2.cloned.1.call-done = bf16[32,2,1024,512]{3,2,0,1:T(8,128)(2,1)} async-done(((bf16[32,2,1024,256]{3,2,0,1:T(8,128)(2,1)}), bf16[32,2,1024,512]{3,2,0,1:T(8,128)(2,1)}) %all-gather.2.cloned.1.call-update) | async-done | bytes 67108880 | tf_op jit(solution)/shard_map/all_gather | solution.py:75
  800.2 19.6 %fusion.1 = f32[32,128,512]{2,1,0:T(8,128)} fusion(bf16[32,2,1024,512]{3,2,0,1:T(8,128)(2,1)} %all-gather.2.cloned.1.call-done, bf16[2,32,2048,128]{2,3,1,0:T(8,128)(2,1)} %slice_dynamic-update-slice_fusion.1, s32[]{:T(128)S(6)} %select_n.202), kind=kOutput, calls=%fused_computation.13 | convolution fusion | flops 4294967296 | bytes 50331652 | tf_op jit(solution)/shard_map/cab,cas->cbs/dot_general | solution.py:46
  819.8 19.4 %fusion.3 = f32[32,128,512]{2,1,0:T(8,128)} fusion(bf16[32,2,1024,512]{3,2,0,1:T(8,128)(2,1)} %all-gather.2.cloned.1.call-done, bf16[2,32,2048,128]{2,3,1,0:T(8,128)(2,1)} %slice_dynamic-update-slice_fusion.1, s32[]{:T(128)S(6)} %add.256, s32[]{:T(128)S(6)} %select_n.202), kind=kOutput, calls=%fused_computation.15 | convolution fusion | flops 4294967296 | bytes 50331656 | tf_op jit(solution)/shard_map/cab,cas->cbs/dot_general | solution.py:46
  839.2 19.4 %fusion = f32[32,128,512]{2,1,0:T(8,128)} fusion(bf16[32,2,1024,512]{3,2,0,1:T(8,128)(2,1)} %all-gather.2.cloned.1.call-done, bf16[2,32,2048,128]{2,3,1,0:T(8,128)(2,1)} %slice_dynamic-update-slice_fusion.1, s32[]{:T(128)S(6)} %add.256, s32[]{:T(128)S(6)} %select_n.202), kind=kOutput, calls=%fused_computation.12 | convolution fusion | flops 4294967296 | bytes 50331656 | tf_op jit(solution)/shard_map/cab,cas->cbs/dot_general | solution.py:46
  858.6 23.9 %fusion.10 = bf16[32,512,128]{1,2,0:T(8,128)(2,1)} fusion(f32[32,128,512]{2,1,0:T(8,128)} %fusion, f32[32,128,512]{2,1,0:T(8,128)} %fusion.1, f32[32,128,512]{2,1,0:T(8,128)} %fusion.3, bf16[32,2,1024,512]{3,2,0,1:T(8,128)(2,1)} %all-gather.2.cloned.1.call-done, bf16[2,32,2048,128]{2,3,1,0:T(8,128)(2,1)} %slice_dynamic-update-slice_fusion.1, s32[]{:T(128)S(6)} %select_n.202), kind=kOutput, calls=%fused_computation.24 | convolution fusion | flops 4307550208 | bytes 71303168 | tf_op jit(solution)/shard_map/cab,cas->cbs/dot_general | solution.py:46
  889.4 14.7 copy.39
  912.5 11.5 reduce-scatter.4.cloned.1.call-done
  935.5 25.4 %all-to-all-done = bf16[32,2,128,128]{2,3,0,1:T(8,128)(2,1)S(1)} async-done(((bf16[32,2,128,128]{2,3,0,1:T(8,128)(2,1)}), bf16[32,2,128,128]{2,3,0,1:T(8,128)(2,1)S(1)}, u32[]{:S(2)}, u32[]{:S(2)}) %all-to-all-start) | async-done | bytes 2097184 | tf_op jit(solution)/shard_map/all_to_all | solution.py:83
  979.7 11.6 slice.174
  991.2 10.0 slice.173
  1018.6 21.3 %slice.178 = f32[4,4,128,256]{2,0,3,1:T(4,128)} slice(f32[8,4,128,256]{2,0,3,1:T(8,128)} %bitcast_add_fusion.4), slice={[1:8:2], [0:4:1], [0:128:1], [0:256:1]} | slice | bytes 4194304 | tf_op jit(solution)/shard_map/slice | solution.py:36
  1040.0 19.6 %slice.177 = f32[4,4,128,256]{2,0,3,1:T(4,128)S(1)} slice(f32[8,4,128,256]{2,0,3,1:T(8,128)} %bitcast_add_fusion.4), slice={[0:8:2], [0:4:1], [0:128:1], [0:256:1]} | slice | bytes 4194304 | tf_op jit(solution)/shard_map/slice | solution.py:35
  1067.6 9.0 gather_fusion.2
  1081.6 39.5 %slice.182 = f32[2,8,128,256]{2,0,3,1:T(2,128)} slice(f32[4,8,128,256]{2,0,3,1:T(4,128)} %bitcast_add_fusion.3), slice={[1:4:2], [0:8:1], [0:128:1], [0:256:1]} | slice | bytes 4194304 | tf_op jit(solution)/shard_map/slice | solution.py:36
  1121.1 36.5 %slice.181 = f32[2,8,128,256]{2,0,3,1:T(2,128)S(1)} slice(f32[4,8,128,256]{2,0,3,1:T(4,128)} %bitcast_add_fusion.3), slice={[0:4:2], [0:8:1], [0:128:1], [0:256:1]} | slice | bytes 4194304 | tf_op jit(solution)/shard_map/slice | solution.py:35
  1163.3 9.6 concatenate.81
  1172.9 11.9 gather_fusion.3
  1202.6 10.3 gather_fusion.4
  1222.2 45.4 %collective-permute-done.7 = f32[16,128,256]{1,0,2:T(8,128)} collective-permute-done((f32[16,128,256]{1,0,2:T(8,128)S(1)}, f32[16,128,256]{1,0,2:T(8,128)}, u32[]{:S(2)}, u32[]{:S(2)}) %collective-permute-start.7) | collective-permute-done | bytes 2097184 | tf_op jit(solution)/shard_map/ppermute | solution.py:11
  1279.0 10.1 gather_fusion.5
  1298.7 44.6 %collective-permute-done.8 = f32[16,128,256]{1,0,2:T(8,128)} collective-permute-done((f32[16,128,256]{1,0,2:T(8,128)S(1)}, f32[16,128,256]{1,0,2:T(8,128)}, u32[]{:S(2)}, u32[]{:S(2)}) %collective-permute-start.8) | collective-permute-done | bytes 2097184 | tf_op jit(solution)/shard_map/ppermute | solution.py:11
  1354.7 10.1 gather_fusion.6
  1372.7 88.8 %collective-permute-done.9 = f32[16,128,256]{1,0,2:T(8,128)S(1)} collective-permute-done((f32[16,128,256]{1,0,2:T(8,128)S(1)}, f32[16,128,256]{1,0,2:T(8,128)S(1)}, u32[]{:S(2)}, u32[]{:S(2)}) %collective-permute-start.9) | collective-permute-done | bytes 2097184 | tf_op jit(solution)/shard_map/ppermute | solution.py:11
  1470.1 10.1 gather_fusion.7
  (110 shorter events, 239.9 us)
Async XLA Ops:
  6.5 793.7 %all-gather.2.cloned.1.call-start = ((), (), s32[]{:S(2)}) async-start(), calls=%async_computation.2 | async-start | bytes 100663296 | tf_op jit(solution)/shard_map/all_gather | solution.py:75
  29.4 894.6 %reduce-scatter.4.cloned.1.call-start = ((), (), s32[]{:S(2)}) async-start(), calls=%async_computation.3 | async-start | bytes 6291456
  92.4 9.3 copy-start
  101.6 52.3 %collective-permute-start = (bf16[2,32,128,128]{2,3,1,0:T(8,128)(2,1)S(1)}, bf16[2,32,128,128]{2,3,1,0:T(8,128)(2,1)S(1)}, u32[]{:S(2)}, u32[]{:S(2)}) collective-permute-start(bf16[2,32,128,128]{2,3,1,0:T(8,128)(2,1)S(1)} %get-tuple-element.11), channel_id=1, source_target_pairs={{0,28},{4,0},{8,4},{12,8},{16,12},{20,16},{24,20},{28,24},{1,29},{... | collective-permute-start | bytes 6291464 | tf_op jit(solution)/shard_map/ppermute | solution.py:72
  107.8 91.0 %collective-permute-start.1 = (bf16[2,32,128,128]{2,3,1,0:T(8,128)(2,1)S(1)}, bf16[2,32,128,128]{2,3,1,0:T(8,128)(2,1)}, u32[]{:S(2)}, u32[]{:S(2)}) collective-permute-start(bf16[2,32,128,128]{2,3,1,0:T(8,128)(2,1)S(1)} %get-tuple-element.10), channel_id=1, source_target_pairs={{0,24},{4,28},{8,0},{12,4},{16,8},{20,12},{24,16},{28,20},{1,25},{... | collective-permute-start | bytes 6291464 | tf_op jit(solution)/shard_map/ppermute | solution.py:72
  108.3 135.7 %collective-permute-start.2 = (bf16[2,32,128,128]{2,3,1,0:T(8,128)(2,1)}, bf16[2,32,128,128]{2,3,1,0:T(8,128)(2,1)}, u32[]{:S(2)}, u32[]{:S(2)}) collective-permute-start(bf16[2,32,128,128]{2,3,1,0:T(8,128)(2,1)} %get-tuple-element.9), channel_id=1, source_target_pairs={{0,20},{4,24},{8,28},{12,0},{16,4},{20,8},{24,12},{28,16},{1,21},{... | collective-permute-start | bytes 6291464 | tf_op jit(solution)/shard_map/ppermute | solution.py:72
  108.3 358.5 %collective-permute-start.3 = (bf16[2,32,128,128]{2,3,1,0:T(8,128)(2,1)}, bf16[2,32,128,128]{2,3,1,0:T(8,128)(2,1)}, u32[]{:S(2)}, u32[]{:S(2)}) collective-permute-start(bf16[2,32,128,128]{2,3,1,0:T(8,128)(2,1)} %get-tuple-element.8), channel_id=1, source_target_pairs={{0,16},{4,20},{8,24},{12,28},{16,0},{20,4},{24,8},{28,12},{1,17},{... | collective-permute-start | bytes 6291464 | tf_op jit(solution)/shard_map/ppermute | solution.py:72
  111.3 358.7 %collective-permute-start.4 = (bf16[2,32,128,128]{2,3,1,0:T(8,128)(2,1)}, bf16[2,32,128,128]{2,3,1,0:T(8,128)(2,1)}, u32[]{:S(2)}, u32[]{:S(2)}) collective-permute-start(bf16[2,32,128,128]{2,3,1,0:T(8,128)(2,1)} %get-tuple-element.7), channel_id=1, source_target_pairs={{0,12},{4,16},{8,20},{12,24},{16,28},{20,0},{24,4},{28,8},{1,13},{... | collective-permute-start | bytes 6291464 | tf_op jit(solution)/shard_map/ppermute | solution.py:72
  153.9 319.4 %collective-permute-start.5 = (bf16[2,32,128,128]{2,3,1,0:T(8,128)(2,1)}, bf16[2,32,128,128]{2,3,1,0:T(8,128)(2,1)}, u32[]{:S(2)}, u32[]{:S(2)}) collective-permute-start(bf16[2,32,128,128]{2,3,1,0:T(8,128)(2,1)} %get-tuple-element.6), channel_id=1, source_target_pairs={{0,8},{4,12},{8,16},{12,20},{16,24},{20,28},{24,0},{28,4},{1,9},{5... | collective-permute-start | bytes 6291464 | tf_op jit(solution)/shard_map/ppermute | solution.py:72
  198.9 277.8 %collective-permute-start.6 = (bf16[2,32,128,128]{2,3,1,0:T(8,128)(2,1)}, bf16[2,32,128,128]{2,3,1,0:T(8,128)(2,1)}, u32[]{:S(2)}, u32[]{:S(2)}) collective-permute-start(bf16[2,32,128,128]{2,3,1,0:T(8,128)(2,1)} %get-tuple-element.5), channel_id=1, source_target_pairs={{0,4},{4,8},{8,12},{12,16},{16,20},{20,24},{24,28},{28,0},{1,5},{5... | collective-permute-start | bytes 6291464 | tf_op jit(solution)/shard_map/ppermute | solution.py:72
  911.8 0.7 copy-start.7
  931.3 29.5 %all-to-all-start = ((bf16[32,2,128,128]{2,3,0,1:T(8,128)(2,1)}), bf16[32,2,128,128]{2,3,0,1:T(8,128)(2,1)S(1)}, u32[]{:S(2)}, u32[]{:S(2)}) async-start(bf16[32,2,128,128]{2,3,0,1:T(8,128)(2,1)} %copy.29), calls=%async_computation | async-start | bytes 4194304 | tf_op jit(solution)/shard_map/all_to_all | solution.py:83
  1212.9 4.2 copy-start.6
  1218.1 2.0 copy-start.2
  1220.4 47.2 %collective-permute-start.7 = (f32[16,128,256]{1,0,2:T(8,128)S(1)}, f32[16,128,256]{1,0,2:T(8,128)}, u32[]{:S(2)}, u32[]{:S(2)}) collective-permute-start(f32[16,128,256]{1,0,2:T(8,128)S(1)} %fusion.13), channel_id=1, source_target_pairs={{0,4},{4,0},{8,12},{12,8},{16,20},{20,16},{24,28},{28,24},{1,5},{5... | collective-permute-start | bytes 6291464 | tf_op jit(solution)/shard_map/ppermute | solution.py:11
  1289.1 4.2 copy-start.3
  1294.7 2.0 copy-start.1
  1297.0 46.3 %collective-permute-start.8 = (f32[16,128,256]{1,0,2:T(8,128)S(1)}, f32[16,128,256]{1,0,2:T(8,128)}, u32[]{:S(2)}, u32[]{:S(2)}) collective-permute-start(f32[16,128,256]{1,0,2:T(8,128)S(1)} %slice_select_fusion.4), channel_id=1, source_target_pairs={{0,8},{4,12},{8,0},{12,4},{16,24},{20,28},{24,16},{28,20},{1,9},{5... | collective-permute-start | bytes 6291464 | tf_op jit(solution)/shard_map/ppermute | solution.py:11
  1364.8 4.2 copy-start.4
  1370.3 91.2 %collective-permute-start.9 = (f32[16,128,256]{1,0,2:T(8,128)S(1)}, f32[16,128,256]{1,0,2:T(8,128)S(1)}, u32[]{:S(2)}, u32[]{:S(2)}) collective-permute-start(f32[16,128,256]{1,0,2:T(8,128)S(1)} %slice_select_fusion.1), channel_id=1, source_target_pairs={{0,16},{4,20},{8,24},{12,28},{16,0},{20,4},{24,8},{28,12},{1,17},{... | collective-permute-start | bytes 6291464 | tf_op jit(solution)/shard_map/ppermute | solution.py:11
  1480.3 4.2 copy-start.5
Sparse Core Ops, SparseCore 0:
  29.6 770.6 all-gather.1
  912.0 12.0 reduce-scatter.3
